TPU v7x, 32 devices: a whole 2x2x4 slice. The times are simulated.
32 devices in a mesh: dp: 8 (over y, x, core), mp: 4 (over z).
Axes of the slice: x: 2, y: 2, z: 4, core: 2. Of those that a mesh axis runs over, the one named last changes fastest.
Arguments:
- hidden: bfloat16 [192, 256, 4096], P(('dp', 'mp')), may hold values from -6 to 6
- lengths: int32 [192], P(('dp', 'mp')), may hold values from 32 to 256, as said below
- list_ids: int32 [192], P('dp'), may hold values from 0 to 65535, as said below
- gain: bfloat16 [4096], replicated, may hold values from 0.099609375 to 1.8984375
- head: bfloat16 [4096, 1024], P('dp', 'mp'), may hold values from -0.09375 to 0.09375
- list_slot: int32 [65536], replicated, may hold values from 0 to 65535, as said below
- centroids: bfloat16 [65536, 1024], P('dp'), may hold values from -0.59765625 to 0.59765625
- rotation: bfloat16 [1024, 1024], P('mp'), may hold values from -0.1875 to 0.1875
Outputs:
- codes: bfloat16 [192, 1024], P('dp', 'mp')
- scales: bfloat16 [192, 16], P('dp', 'mp')
Inputs may be any that keep to these rules, and one draw needn't show every extreme that they name: `list_ids`: in each aligned block of 24 passages, at most 6 have lists in one range of 8192 lists (list id // 8192); one range holds exactly 6 of them in every block. Each list's row in the centroid table; list_slot[l] // 8192 equals l // 8192, and each row of a range once. `lengths`: some passage has exactly 256 valid tokens.
All inputs are finite; a program needn't handle non-finite values. Where the computation divides by a largest or mean magnitude, that divisor is 1e-20 or more.
Results may differ from a plain program's by a relative error of at most 0.013.
Values may be sent and summed in bfloat16 or wider, within the bound.
No kernel may reach another device: no remote copies, remote signals or barrier semaphores. Data moves between devices by JAX's collectives and lax.ppermute only.
A program may use at most 64 MiB of HBM per device.

v0:
```python
import jax
import jax.numpy as jnp
from jax import lax
from jax.sharding import PartitionSpec as P

BLOCK = 64


def quantize(rotated):
    lead = rotated.shape[:-1]
    width = rotated.shape[-1]
    blocks = rotated.reshape(lead + (width // BLOCK, BLOCK))
    scale = jnp.max(jnp.abs(blocks), axis=-1) + 1e-06
    codes = (blocks / scale[..., None]).reshape(lead + (width,)).astype(jnp.bfloat16)
    return (codes, scale.astype(jnp.bfloat16))


def pick_own(placing, buckets):
    picked = jnp.einsum("poc,oce->pe", placing, buckets, preferred_element_type=jnp.float32)
    return picked.astype(buckets.dtype)


def per_device(hidden, lengths, list_ids, gain, head, list_slot, centroids, rotation):
    passes, slots, width = hidden.shape
    states = hidden.astype(jnp.float32)
    mean_square = jnp.mean(states * states, axis=-1)
    valid = jnp.arange(slots, dtype=jnp.int32)[None, :] < lengths[:, None]
    weights = (
        jnp.where(valid, lax.rsqrt(mean_square + 1e-05), 0.0) / lengths.astype(jnp.float32)[:, None]
    )
    pooled_mine = (jnp.einsum("pl,pld->pd", weights, states) * gain.astype(jnp.float32)).astype(
        jnp.bfloat16
    )
    pooled = lax.all_gather(pooled_mine, "mp", axis=0, tiled=True)
    group = pooled.shape[0]
    col_width = head.shape[1]
    projected = jnp.dot(
        pooled, lax.all_gather(head, "dp", axis=0, tiled=True), preferred_element_type=jnp.float32
    ).astype(jnp.bfloat16)
    owners = lax.axis_size("dp")
    lists_own = centroids.shape[0]
    capacity = max(2, 2 * group // owners)
    col_start = lax.axis_index("mp") * col_width
    cent_cols = lax.dynamic_slice_in_dim(centroids, col_start, col_width, 1)
    owner = list_ids // lists_own
    local_row = list_slot[list_ids] % lists_own
    matches = (owner[:, None] == jnp.arange(owners, dtype=jnp.int32)[None, :]).astype(jnp.int32)
    earlier = jnp.cumsum(matches, axis=0) - matches
    rank = jnp.sum(earlier * matches, axis=1)
    placed = (matches[:, :, None] > 0) & (
        rank[:, None, None] == jnp.arange(capacity, dtype=jnp.int32)[None, None, :]
    )
    placing = placed.astype(jnp.bfloat16)
    bucket_ids = jnp.sum(jnp.where(placed, local_row[:, None, None], 0), axis=0)
    cents_back = lax.all_to_all(
        cent_cols[lax.all_to_all(bucket_ids, "dp", split_axis=0, concat_axis=0, tiled=True)],
        "dp",
        split_axis=0,
        concat_axis=0,
        tiled=True,
    )
    cents = pick_own(placing, cents_back)
    resid = (projected.astype(jnp.float32) - cents.astype(jnp.float32)).astype(jnp.bfloat16)
    partial_value = jnp.dot(resid, rotation, preferred_element_type=jnp.float32)
    rotated = lax.psum_scatter(partial_value, "mp", scatter_dimension=1, tiled=True)
    codes, scales = quantize(rotated)
    return (codes, scales)


def solution(mesh):
    in_specs = (
        P(("dp", "mp"), None, None),
        P(("dp", "mp")),
        P("dp"),
        P(),
        P("dp", "mp"),
        P(),
        P("dp", None),
        P("mp", None),
    )
    out_specs = (P("dp", "mp"), P("dp", "mp"))
    return jax.shard_map(
        per_device, mesh=mesh, in_specs=in_specs, out_specs=out_specs, check_vma=False
    )
```

profile of v0, /device:TPU:0, one launch (start us, length us, event | category | flops | bytes accessed | tf_op | source)
XLA Modules:
  0.0 92.6 jit_solution(1821076101298347327)
XLA Ops:
  7.2 0.0 copy-start
  7.2 0.0 copy-start.2
  7.2 0.0 copy-start.1
  7.2 0.7 and_select_fusion.2
  7.9 0.1 fusion.16
  8.0 0.2 select_reduce_fusion
  8.2 0.1 copy.16
  8.3 1.7 %gather_fusion = s32[24]{0:T(128)S(1)} fusion(s32[65536]{0:T(1024)} %param.13, s32[1024]{0:T(1024)S(1)} %pad_clamp_fusion.1), kind=kCustom, calls=%fused_computation | custom fusion | bytes 288 | tf_op jit(solution)/shard_map/gather | solution.py:46
  10.0 0.8 fusion.10
  10.8 5.2 %all-to-all-start = ((s32[8,1,6]{2,1,0:T(1,128)}), s32[8,1,6]{2,1,0:T(1,128)S(1)}, u32[]{:S(2)}, u32[]{:S(2)}) async-start(s32[8,1,6]{2,1,0:T(1,128)} %bitcast.4), calls=%async_computation | async-start | bytes 8192 | tf_op jit(solution)/shard_map/all_to_all | solution.py:56
  16.0 0.0 all-gather.3.cloned.1.call-start
  16.1 0.7 all-gather.3.cloned.1.call-update
  16.7 7.1 %multiply_reduce_fusion = f32[6,256]{1,0:T(8,128)S(1)} fusion(bf16[6,256,4096]{2,1,0:T(8,128)(2,1)} %param.8), kind=kLoop, calls=%fused_computation.2 | loop fusion | flops 18872832 | bytes 12589056 | tf_op jit(solution)/shard_map/reduce_sum | solution.py:26
  23.8 0.0 copy-done.2
  23.8 0.0 copy-done.1
  23.9 0.1 divide_bitcast_fusion
  23.9 6.5 %fusion.17 = f32[6,1,4096]{2,1,0:T(1,128)S(1)} fusion(bf16[6,256,4096]{2,1,0:T(8,128)(2,1)} %param.8, bf16[6,256,1]{1,0,2:T(8,128)(2,1)S(1)} %divide_bitcast_fusion), kind=kOutput, calls=%fused_computation.27 | convolution fusion | flops 12582912 | bytes 12684288 | tf_op jit(solution)/shard_map/pl,pld->pd/dot_general | solution.py:31
  30.4 0.1 fusion.7
  30.5 4.4 %constant_dynamic-slice_fusion = bf16[8192,256]{1,0:T(8,128)(2,1)} fusion(bf16[8192,1024]{1,0:T(8,128)(2,1)} %param.14, s32[]{:T(128)S(6)} %select_n.42), kind=kLoop, calls=%fused_computation.42 | loop fusion | bytes 8388612 | tf_op jit(solution)/shard_map/dynamic_slice | solution.py:44
  34.9 14.2 %all-gather = bf16[4,6,4096]{2,1,0:T(8,128)(2,1)S(1)} all-gather(bf16[1,6,4096]{2,1,0:T(8,128)(2,1)S(1)} %fusion.7), channel_id=1, replica_groups=mesh['dp'=8,'mp'=4] {'mp'}, dimensions={0}, use_global_device_ids=true | all-gather | bytes 245760 | tf_op jit(solution)/shard_map/all_gather | solution.py:34
  49.1 0.1 reshape.121
  49.2 0.0 all-to-all-done
  49.2 0.1 copy.18
  49.3 0.1 copy.19
  49.4 0.1 reshape.112
  49.5 3.4 %gather_fusion.1 = bf16[48,256]{1,0:T(8,128)(2,1)S(1)} fusion(bf16[8192,256]{1,0:T(8,128)(2,1)} %constant_dynamic-slice_fusion, s32[1024]{0:T(1024)S(1)} %pad_clamp_fusion), kind=kCustom, calls=%fused_computation.1 | custom fusion | bytes 49344 | tf_op jit(solution)/shard_map/gather | solution.py:56
  52.9 0.6 reshape.111
  53.5 4.0 %all-to-all-start.1 = ((bf16[8,6,256]{2,1,0:T(8,128)(2,1)}), bf16[8,6,256]{2,1,0:T(8,128)(2,1)S(1)}, u32[]{:S(2)}, u32[]{:S(2)}) async-start(bf16[8,6,256]{2,1,0:T(8,128)(2,1)} %reshape.111), calls=%async_computation.1 | async-start | bytes 65536 | tf_op jit(solution)/shard_map/all_to_all | solution.py:55
  57.5 0.0 reduce-scatter.2.cloned.1.call-start
  57.5 0.0 all-gather.3.cloned.1.call-done
  57.5 2.0 %fusion.4 = f32[24,256]{1,0:T(8,128)S(1)} fusion(bf16[24,4096]{1,0:T(8,128)(2,1)S(1)} %reshape.121, bf16[4096,256]{1,0:T(8,128)(2,1)} %all-gather.3.cloned.1.call-done), kind=kOutput, calls=%fused_computation.9 | convolution fusion | flops 50343936 | bytes 2318336 | tf_op jit(solution)/shard_map/dot_general | solution.py:37
  59.5 2.8 %all-to-all-done.1 = bf16[8,6,256]{2,1,0:T(8,128)(2,1)S(1)} async-done(((bf16[8,6,256]{2,1,0:T(8,128)(2,1)}), bf16[8,6,256]{2,1,0:T(8,128)(2,1)S(1)}, u32[]{:S(2)}, u32[]{:S(2)}) %all-to-all-start.1) | async-done | bytes 24608 | tf_op jit(solution)/shard_map/all_to_all | solution.py:55
  62.3 0.0 copy-done
  62.3 1.0 %fusion.5 = f32[24,1024]{1,0:T(8,128)} fusion(bf16[256,1024]{1,0:T(8,128)(2,1)S(1)} %copy-done, f32[24,256]{1,0:T(8,128)S(1)} %fusion.4, bf16[8,6,256]{2,1,0:T(8,128)(2,1)S(1)} %all-to-all-done.1, pred[24,6]{0,1:T(8,128)(4,1)S(1)} %iota_compare_fusion.2, pred[24,8]{0,1:T(8,128)(4,1)S(1)} %copy.16), kind=kOutput, calls=%fused_computation.10 | convolution fusion | flops 13198464 | bytes 672080 | tf_op jit(solution)/shard_map/dot_general | solution.py:64
  63.3 0.0 reduce-scatter.2.cloned.1.call-update
  63.3 19.3 %reduce-scatter.2.cloned.1.call-done = f32[24,256]{1,0:T(8,128)} async-done(((f32[24,1024]{1,0:T(8,128)}), f32[24,256]{1,0:T(8,128)}) %reduce-scatter.2.cloned.1.call-update) | async-done | bytes 24592 | tf_op jit(solution)/shard_map/reduce_scatter | solution.py:65
  82.6 0.7 abs.6
  83.3 0.1 abs.7
  83.4 0.1 reduce_max.9
  83.5 0.1 div.45
  83.6 0.1 div.46
  83.7 0.7 copy.20
  84.4 1.3 %divide_convert_fusion = bf16[24,256]{1,0:T(8,128)(2,1)} fusion(f32[24,256]{1,0:T(8,128)} %reduce-scatter.2.cloned.1.call-done, f32[24,256]{1,0:T(8,128)S(1)} %div.46), kind=kLoop, calls=%fused_computation.17 | loop fusion | flops 12288 | bytes 61440 | tf_op jit(solution)/shard_map/convert_element_type | solution.py:14
  (9 shorter events, 0.1 us)
Async XLA Ops:
  7.2 55.2 %copy-start = (bf16[256,1024]{1,0:T(8,128)(2,1)S(1)}, bf16[256,1024]{1,0:T(8,128)(2,1)}, u32[]{:S(2)}) copy-start(bf16[256,1024]{1,0:T(8,128)(2,1)} %param.15) | copy-start | bytes 1572868
  7.2 16.6 %copy-start.2 = (s32[6]{0:T(128)S(1)}, s32[6]{0:T(128)}, u32[]{:S(2)}) copy-start(s32[6]{0:T(128)} %param.9) | copy-start | bytes 76
  7.2 16.6 %copy-start.1 = (bf16[4096]{0:T(1024)(128)(2,1)S(1)}, bf16[4096]{0:T(1024)(128)(2,1)}, u32[]{:S(2)}) copy-start(bf16[4096]{0:T(1024)(128)(2,1)} %param.11) | copy-start | bytes 24580
  10.8 38.4 %all-to-all-start = ((s32[8,1,6]{2,1,0:T(1,128)}), s32[8,1,6]{2,1,0:T(1,128)S(1)}, u32[]{:S(2)}, u32[]{:S(2)}) async-start(s32[8,1,6]{2,1,0:T(1,128)} %bitcast.4), calls=%async_computation | async-start | bytes 8192 | tf_op jit(solution)/shard_map/all_to_all | solution.py:56
  16.0 41.5 %all-gather.3.cloned.1.call-start = ((), (), s32[]{:S(2)}) async-start(), calls=%async_computation.3 | async-start | bytes 2359296 | tf_op jit(solution)/shard_map/all_gather | solution.py:38
  53.5 8.8 %all-to-all-start.1 = ((bf16[8,6,256]{2,1,0:T(8,128)(2,1)}), bf16[8,6,256]{2,1,0:T(8,128)(2,1)S(1)}, u32[]{:S(2)}, u32[]{:S(2)}) async-start(bf16[8,6,256]{2,1,0:T(8,128)(2,1)} %reshape.111), calls=%async_computation.1 | async-start | bytes 65536 | tf_op jit(solution)/shard_map/all_to_all | solution.py:55
  57.5 25.1 %reduce-scatter.2.cloned.1.call-start = ((), (), s32[]{:S(2)}) async-start(), calls=%async_computation.4 | async-start | bytes 122880 | tf_op jit(solution)/shard_map/reduce_scatter | solution.py:65
Sparse Core Ops, SparseCore 0:
  18.7 29.4 all-gather.2
  63.4 19.0 reduce-scatter.1
where the time goes:
time: 93.2 us; the launch traced here: 92.6 us
  waiting for transfers between devices  22.8 us (24%)
  blocking collectives  14.2 us (15%)
  between operations  14.2 us (15%)
  local copies, waits for them, and re-layouts  11.4 us (12%)
  other arithmetic  11.3 us (12%)
  matrix products  9.46 us (10%)
  starting transfers between devices  9.28 us (10%)
    reduce_scatter x1, waiting for transfers between devices, per_device(): lax.psum_scatter(partial_value, 'mp', scatter_dimension=1, tiled=True)  19.3 us
    all_gather x1, blocking collectives, per_device(): pooled = lax.all_gather(pooled_mine, 'mp', axis=0, tiled=True)  14.2 us
    reduce_sum x1, other arithmetic, per_device(): mean_square = jnp.mean(states * states, axis=-1)  7.07 us
    dot_general x1, matrix products, per_device(): jnp.einsum('pl,pld->pd', weights, states) * gain.astype(jnp.float32)  6.5 us
    all_to_all x1, starting transfers between devices, per_device(): lax.all_to_all(bucket_ids, 'dp', split_axis=0, concat_axis=0, tiled=True)  5.2 us
    dynamic_slice x1, local copies, waits for them, and re-layouts, per_device(): cent_cols = lax.dynamic_slice_in_dim(centroids, col_start, col_width, 1)  4.4 us
    all_to_all x1, starting transfers between devices, per_device(): lax.all_to_all(cent_cols[lax.all_to_all(bucket_ids, 'dp', split_axis=0, c...  4.01 us
    gather x2, local copies, waits for them, and re-layouts, per_device(): cent_cols[lax.all_to_all(bucket_ids, 'dp', split_axis=0, concat_axis=0, t...  3.97 us
  transfers between devices with their start and end apart: 4, of which 2 were waited for; matrix products, arithmetic and copies ran while one was open for 26% of the time, Pallas kernels for 0%

commit v1 on v0

--- a/solution.py
+++ b/solution.py
@@ -4,6 +4,19 @@
 from jax.sharding import PartitionSpec as P
 
 BLOCK = 64
+
+
+def gather_around(shard, axis, dim):
+    ways = lax.axis_size(axis)
+    up = [(d, (d + 1) % ways) for d in range(ways)]
+    down = [(d, (d - 1) % ways) for d in range(ways)]
+    earlier, later = ([shard], [shard])
+    for _ in range(ways // 2):
+        earlier.append(lax.ppermute(earlier[-1], axis, up))
+    for _ in range((ways - 1) // 2):
+        later.append(lax.ppermute(later[-1], axis, down))
+    line = jnp.concatenate([*earlier[::-1], *later[1:]], axis=dim)
+    return jnp.roll(line, (lax.axis_index(axis) - ways // 2) * shard.shape[dim], axis=dim)
 
 
 def quantize(rotated):
@@ -31,7 +44,7 @@
     pooled_mine = (jnp.einsum("pl,pld->pd", weights, states) * gain.astype(jnp.float32)).astype(
         jnp.bfloat16
     )
-    pooled = lax.all_gather(pooled_mine, "mp", axis=0, tiled=True)
+    pooled = gather_around(pooled_mine, "mp", 0)
     group = pooled.shape[0]
     col_width = head.shape[1]
     projected = jnp.dot(

time: 93.2 us -> 86.6 us (0.929)
  blocking collectives: 14.2 us -> 0 us
  starting transfers between devices: 9.28 us -> 13.4 us
  waiting for transfers between devices: 22.8 us -> 25.5 us
    all_gather x1 -> x0, blocking collectives: 14.2 us -> none  [per_device(): pooled = lax.all_gather(pooled_mine, 'mp', axis=0, tiled=True)]
    ppermute x0 -> x3, starting transfers between devices: none -> 3.84 us  [the longest x1 2.22 us: gather_around(): later.append(lax.ppermute(later[-1], axis, down))]
    ppermute x0 -> x3, waiting for transfers between devices: none -> 3.29 us  [the longest x2 3.29 us: gather_around(): earlier.append(lax.ppermute(earlier[-1], axis, up))]
    dot_general x1, matrix products: 0.98 us -> 2.92 us  [per_device(): partial_value = jnp.dot(resid, rotation, preferred_element_type=jnp.float32)]
    dot_general x1, matrix products: 1.98 us -> 0.2 us  [pick_own(): jnp.einsum('poc,oce->pe', placing, buckets, preferred_element_type=jnp.fl...]
  transfers between devices with their start and end apart: 4 -> 7, of which waited for: 2 -> 3; matrix products, arithmetic and copies ran while one was open for 26% -> 27% of each run, Pallas kernels for 0% -> 0%
where the time goes in v1:
time: 86.6 us; the launch traced here: 86.1 us
  waiting for transfers between devices  25.5 us (29%)
  between operations  14.2 us (16%)
  starting transfers between devices  13.4 us (15%)
  local copies, waits for them, and re-layouts  12.1 us (14%)
  other arithmetic  11.3 us (13%)
  matrix products  9.62 us (11%)
    reduce_scatter x1, waiting for transfers between devices, per_device(): lax.psum_scatter(partial_value, 'mp', scatter_dimension=1, tiled=True)  18.9 us
    reduce_sum x1, other arithmetic, per_device(): mean_square = jnp.mean(states * states, axis=-1)  7.07 us
    dot_general x1, matrix products, per_device(): jnp.einsum('pl,pld->pd', weights, states) * gain.astype(jnp.float32)  6.5 us
    all_to_all x1, starting transfers between devices, per_device(): lax.all_to_all(bucket_ids, 'dp', split_axis=0, concat_axis=0, tiled=True)  5.2 us
    dynamic_slice x1, local copies, waits for them, and re-layouts, per_device(): cent_cols = lax.dynamic_slice_in_dim(centroids, col_start, col_width, 1)  4.4 us
    all_to_all x1, starting transfers between devices, per_device(): lax.all_to_all(cent_cols[lax.all_to_all(bucket_ids, 'dp', split_axis=0, c...  4.28 us
    gather x2, local copies, waits for them, and re-layouts, per_device(): cent_cols[lax.all_to_all(bucket_ids, 'dp', split_axis=0, concat_axis=0, t...  3.97 us
    ppermute x2, waiting for transfers between devices, gather_around(): earlier.append(lax.ppermute(earlier[-1], axis, up))  3.29 us
  transfers between devices with their start and end apart: 7, of which 3 were waited for; matrix products, arithmetic and copies ran while one was open for 27% of the time, Pallas kernels for 0%

profile of v1, /device:TPU:0, one launch (start us, length us, event | category | flops | bytes accessed | tf_op | source)
XLA Modules:
  0.0 86.1 jit_solution(13283783007853853963)
XLA Ops:
  7.2 0.0 copy-start
  7.2 0.0 copy-start.2
  7.2 0.0 copy-start.1
  7.2 0.7 and_select_fusion.2
  7.9 0.1 fusion.14
  8.0 0.2 select_reduce_fusion
  8.2 0.1 copy.16
  8.3 1.7 %gather_fusion = s32[24]{0:T(128)S(1)} fusion(s32[65536]{0:T(1024)} %param.13, s32[1024]{0:T(1024)S(1)} %pad_clamp_fusion.1), kind=kCustom, calls=%fused_computation | custom fusion | bytes 288 | tf_op jit(solution)/shard_map/gather | solution.py:59
  10.0 0.8 fusion.10
  10.8 5.2 %all-to-all-start = ((s32[8,1,6]{2,1,0:T(1,128)}), s32[8,1,6]{2,1,0:T(1,128)S(1)}, u32[]{:S(2)}, u32[]{:S(2)}) async-start(s32[8,1,6]{2,1,0:T(1,128)} %bitcast.3), calls=%async_computation | async-start | bytes 8192 | tf_op jit(solution)/shard_map/all_to_all | solution.py:69
  16.0 0.0 all-gather.2.cloned.1.call-start
  16.1 0.7 all-gather.2.cloned.1.call-update
  16.7 7.1 %multiply_reduce_fusion = f32[6,256]{1,0:T(8,128)S(1)} fusion(bf16[6,256,4096]{2,1,0:T(8,128)(2,1)} %param.8), kind=kLoop, calls=%fused_computation.2 | loop fusion | flops 18872832 | bytes 12589056 | tf_op jit(solution)/shard_map/reduce_sum | solution.py:39
  23.8 0.0 copy-done.2
  23.8 0.0 copy-done.1
  23.8 0.1 divide_bitcast_fusion
  23.9 6.5 %fusion.15 = f32[6,1,4096]{2,1,0:T(1,128)S(1)} fusion(bf16[6,256,4096]{2,1,0:T(8,128)(2,1)} %param.8, bf16[6,256,1]{1,0,2:T(8,128)(2,1)S(1)} %divide_bitcast_fusion), kind=kOutput, calls=%fused_computation.27 | convolution fusion | flops 12582912 | bytes 12684288 | tf_op jit(solution)/shard_map/pl,pld->pd/dot_general | solution.py:44
  30.4 0.1 fusion.8
  30.5 1.6 %collective-permute-start = (bf16[6,4096]{1,0:T(8,128)(2,1)S(1)}, bf16[6,4096]{1,0:T(8,128)(2,1)S(1)}, u32[]{:S(2)}, u32[]{:S(2)}) collective-permute-start(bf16[6,4096]{1,0:T(8,128)(2,1)S(1)} %fusion.8), channel_id=1, source_target_pairs={{0,1},{1,2},{2,3},{3,0},{4,5},{5,6},{6,7},{7,4},{8,9},{9,10},{10,1... | collective-permute-start | bytes 147464 | tf_op jit(solution)/shard_map/ppermute | solution.py:15
  32.1 4.4 %constant_dynamic-slice_fusion = bf16[8192,256]{1,0:T(8,128)(2,1)} fusion(bf16[8192,1024]{1,0:T(8,128)(2,1)} %param.14, s32[]{:T(128)S(6)} %select_n.56), kind=kLoop, calls=%fused_computation.42 | loop fusion | bytes 8388612 | tf_op jit(solution)/shard_map/dynamic_slice | solution.py:57
  36.5 0.0 all-to-all-done
  36.5 0.1 copy.18
  36.6 0.1 copy.19
  36.7 0.1 reshape.112
  36.8 3.4 %gather_fusion.1 = bf16[48,256]{1,0:T(8,128)(2,1)S(1)} fusion(bf16[8192,256]{1,0:T(8,128)(2,1)} %constant_dynamic-slice_fusion, s32[1024]{0:T(1024)S(1)} %pad_clamp_fusion), kind=kCustom, calls=%fused_computation.1 | custom fusion | bytes 49344 | tf_op jit(solution)/shard_map/gather | solution.py:69
  40.1 0.6 reshape.111
  40.8 4.3 %all-to-all-start.1 = ((bf16[8,6,256]{2,1,0:T(8,128)(2,1)}), bf16[8,6,256]{2,1,0:T(8,128)(2,1)S(1)}, u32[]{:S(2)}, u32[]{:S(2)}) async-start(bf16[8,6,256]{2,1,0:T(8,128)(2,1)} %reshape.111), calls=%async_computation.1 | async-start | bytes 65536 | tf_op jit(solution)/shard_map/all_to_all | solution.py:68
  45.0 0.0 reduce-scatter.2.cloned.1.call-start
  45.1 2.2 %collective-permute-start.2 = (bf16[6,4096]{1,0:T(8,128)(2,1)S(1)}, bf16[6,4096]{1,0:T(8,128)(2,1)S(1)}, u32[]{:S(2)}, u32[]{:S(2)}) collective-permute-start(bf16[6,4096]{1,0:T(8,128)(2,1)S(1)} %fusion.8), channel_id=1, source_target_pairs={{0,3},{1,0},{2,1},{3,2},{4,7},{5,4},{6,5},{7,6},{8,11},{9,8},{10,9... | collective-permute-start | bytes 147464 | tf_op jit(solution)/shard_map/ppermute | solution.py:17
  47.3 0.0 collective-permute-done
  47.3 0.0 collective-permute-start.1
  47.3 2.6 %all-to-all-done.1 = bf16[8,6,256]{2,1,0:T(8,128)(2,1)S(1)} async-done(((bf16[8,6,256]{2,1,0:T(8,128)(2,1)}), bf16[8,6,256]{2,1,0:T(8,128)(2,1)S(1)}, u32[]{:S(2)}, u32[]{:S(2)}) %all-to-all-start.1) | async-done | bytes 24608 | tf_op jit(solution)/shard_map/all_to_all | solution.py:68
  49.9 0.2 fusion.1
  50.1 0.0 collective-permute-done.2
  50.1 3.3 %collective-permute-done.1 = bf16[6,4096]{1,0:T(8,128)(2,1)S(1)} collective-permute-done((bf16[6,4096]{1,0:T(8,128)(2,1)S(1)}, bf16[6,4096]{1,0:T(8,128)(2,1)S(1)}, u32[]{:S(2)}, u32[]{:S(2)}) %collective-permute-start.1) | collective-permute-done | bytes 49184 | tf_op jit(solution)/shard_map/ppermute | solution.py:15
  53.4 0.8 concatenate.6
  54.2 0.0 all-gather.2.cloned.1.call-done
  54.2 0.0 copy-done
  54.3 2.9 %fusion.5 = f32[24,1024]{1,0:T(8,128)} fusion(bf16[256,1024]{1,0:T(8,128)(2,1)S(1)} %copy-done, f32[24,256]{1,0:T(8,128)S(1)} %fusion.1, bf16[4096,256]{1,0:T(8,128)(2,1)} %all-gather.2.cloned.1.call-done, bf16[48,4096]{1,0:T(8,128)(2,1)S(1)} %concatenate.6, s32[]{:T(128)S(6)} %select_n.54), kind=kOutput, calls=%fused_computation.10 | convolution fusion | flops 62939136 | bytes 2940932 | tf_op jit(solution)/shard_map/dot_general | solution.py:77
  57.2 0.0 reduce-scatter.2.cloned.1.call-update
  57.2 18.9 %reduce-scatter.2.cloned.1.call-done = f32[24,256]{1,0:T(8,128)} async-done(((f32[24,1024]{1,0:T(8,128)}), f32[24,256]{1,0:T(8,128)}) %reduce-scatter.2.cloned.1.call-update) | async-done | bytes 24592 | tf_op jit(solution)/shard_map/reduce_scatter | solution.py:78
  76.1 0.7 abs.6
  76.8 0.1 abs.7
  76.9 0.1 reduce_max.9
  77.0 0.1 div.45
  77.1 0.1 div.46
  77.2 0.7 copy.20
  77.9 1.3 %divide_convert_fusion = bf16[24,256]{1,0:T(8,128)(2,1)} fusion(f32[24,256]{1,0:T(8,128)} %reduce-scatter.2.cloned.1.call-done, f32[24,256]{1,0:T(8,128)S(1)} %div.46), kind=kLoop, calls=%fused_computation.17 | loop fusion | flops 12288 | bytes 61440 | tf_op jit(solution)/shard_map/convert_element_type | solution.py:27
  (9 shorter events, 0.1 us)
Async XLA Ops:
  7.2 47.1 %copy-start = (bf16[256,1024]{1,0:T(8,128)(2,1)S(1)}, bf16[256,1024]{1,0:T(8,128)(2,1)}, u32[]{:S(2)}) copy-start(bf16[256,1024]{1,0:T(8,128)(2,1)} %param.15) | copy-start | bytes 1572868
  7.2 16.6 %copy-start.2 = (s32[6]{0:T(128)S(1)}, s32[6]{0:T(128)}, u32[]{:S(2)}) copy-start(s32[6]{0:T(128)} %param.9) | copy-start | bytes 76
  7.2 16.6 %copy-start.1 = (bf16[4096]{0:T(1024)(128)(2,1)S(1)}, bf16[4096]{0:T(1024)(128)(2,1)}, u32[]{:S(2)}) copy-start(bf16[4096]{0:T(1024)(128)(2,1)} %param.11) | copy-start | bytes 24580
  10.8 25.7 %all-to-all-start = ((s32[8,1,6]{2,1,0:T(1,128)}), s32[8,1,6]{2,1,0:T(1,128)S(1)}, u32[]{:S(2)}, u32[]{:S(2)}) async-start(s32[8,1,6]{2,1,0:T(1,128)} %bitcast.3), calls=%async_computation | async-start | bytes 8192 | tf_op jit(solution)/shard_map/all_to_all | solution.py:69
  16.0 38.2 %all-gather.2.cloned.1.call-start = ((), (), s32[]{:S(2)}) async-start(), calls=%async_computation.3 | async-start | bytes 2359296 | tf_op jit(solution)/shard_map/all_gather | solution.py:51
  30.5 16.8 %collective-permute-start = (bf16[6,4096]{1,0:T(8,128)(2,1)S(1)}, bf16[6,4096]{1,0:T(8,128)(2,1)S(1)}, u32[]{:S(2)}, u32[]{:S(2)}) collective-permute-start(bf16[6,4096]{1,0:T(8,128)(2,1)S(1)} %fusion.8), channel_id=1, source_target_pairs={{0,1},{1,2},{2,3},{3,0},{4,5},{5,6},{6,7},{7,4},{8,9},{9,10},{10,1... | collective-permute-start | bytes 147464 | tf_op jit(solution)/shard_map/ppermute | solution.py:15
  40.8 9.1 %all-to-all-start.1 = ((bf16[8,6,256]{2,1,0:T(8,128)(2,1)}), bf16[8,6,256]{2,1,0:T(8,128)(2,1)S(1)}, u32[]{:S(2)}, u32[]{:S(2)}) async-start(bf16[8,6,256]{2,1,0:T(8,128)(2,1)} %reshape.111), calls=%async_computation.1 | async-start | bytes 65536 | tf_op jit(solution)/shard_map/all_to_all | solution.py:68
  45.0 31.0 %reduce-scatter.2.cloned.1.call-start = ((), (), s32[]{:S(2)}) async-start(), calls=%async_computation.4 | async-start | bytes 122880 | tf_op jit(solution)/shard_map/reduce_scatter | solution.py:78
  45.1 5.0 %collective-permute-start.2 = (bf16[6,4096]{1,0:T(8,128)(2,1)S(1)}, bf16[6,4096]{1,0:T(8,128)(2,1)S(1)}, u32[]{:S(2)}, u32[]{:S(2)}) collective-permute-start(bf16[6,4096]{1,0:T(8,128)(2,1)S(1)} %fusion.8), channel_id=1, source_target_pairs={{0,3},{1,0},{2,1},{3,2},{4,7},{5,4},{6,5},{7,6},{8,11},{9,8},{10,9... | collective-permute-start | bytes 147464 | tf_op jit(solution)/shard_map/ppermute | solution.py:17
  47.3 6.1 %collective-permute-start.1 = (bf16[6,4096]{1,0:T(8,128)(2,1)S(1)}, bf16[6,4096]{1,0:T(8,128)(2,1)S(1)}, u32[]{:S(2)}, u32[]{:S(2)}) collective-permute-start(bf16[6,4096]{1,0:T(8,128)(2,1)S(1)} %collective-permute-done), channel_id=1, source_target_pairs={{0,1},{1,2},{2,3},{3,0},{4,5},{5,6},{6,7},{7,4},{8,9},{9,10},{10,1... | collective-permute-start | bytes 147464 | tf_op jit(solution)/shard_map/ppermute | solution.py:15
Sparse Core Ops, SparseCore 0:
  18.7 29.4 all-gather.1
  57.3 18.7 reduce-scatter.1
